TPU v7x, 32 devices: a whole 2x2x4 slice. The times are simulated.
32 devices in a mesh: ctx: 8 (over z, x), fsdp: 4 (over y, core).
Axes of the slice: x: 2, y: 2, z: 4, core: 2. Of those that a mesh axis runs over, the one named last changes fastest.
Arguments:
- inputs: bfloat16 [4, 4096, 768], P('fsdp', 'ctx'), may hold values from -6 to 6
- doc_starts: int32 [4, 8], P('fsdp'), may hold values from 0 to 4095, as said below
- qkv_weight: bfloat16 [768, 2304], P('fsdp'), may hold values from -0.21875 to 0.21875
- query_bias: bfloat16 [768], P('fsdp'), may hold values from -3 to 3
- value_bias: bfloat16 [768], P('fsdp'), may hold values from -3 to 3
- out_weight: bfloat16 [768, 768], P('fsdp'), may hold values from -2 to 2
- out_bias: bfloat16 [768], P('fsdp'), may hold values from -2 to 2
- norm1_gain: bfloat16 [768], P('fsdp'), may hold values from 0.25 to 1.75
- norm1_bias: bfloat16 [768], P('fsdp'), may hold values from -2 to 2
- in_weight: bfloat16 [768, 3072], P('fsdp'), may hold values from -0.21875 to 0.21875
- in_bias: bfloat16 [3072], P('fsdp'), may hold values from -3 to 3
- back_weight: bfloat16 [3072, 768], P('fsdp'), may hold values from -0.109375 to 0.109375
- back_bias: bfloat16 [768], P('fsdp'), may hold values from -2 to 2
- norm2_gain: bfloat16 [768], P('fsdp'), may hold values from 0.25 to 1.75
- norm2_bias: bfloat16 [768], P('fsdp'), may hold values from -2 to 2
- cotangent: bfloat16 [4, 4096, 768], P('fsdp', 'ctx'), may hold values from -6 to 6
Outputs:
- output: bfloat16 [4, 4096, 768], P('fsdp', 'ctx')
- input_grad: float32 [4, 4096, 768], P('fsdp', 'ctx')
- qkv_weight_grad: float32 [768, 2304], P('fsdp')
- query_bias_grad: float32 [768], P('fsdp')
- value_bias_grad: float32 [768], P('fsdp')
- out_weight_grad: float32 [768, 768], P('fsdp')
- out_bias_grad: float32 [768], P('fsdp')
- norm1_gain_grad: float32 [768], P('fsdp')
- norm1_bias_grad: float32 [768], P('fsdp')
- in_weight_grad: float32 [768, 3072], P('fsdp')
- in_bias_grad: float32 [3072], P('fsdp')
- back_weight_grad: float32 [3072, 768], P('fsdp')
- back_bias_grad: float32 [768], P('fsdp')
- norm2_gain_grad: float32 [768], P('fsdp')
- norm2_bias_grad: float32 [768], P('fsdp')
Inputs may be any that keep to these rules, and one draw needn't show every extreme that they name: `doc_starts`: row s lists the first positions of the 8 documents of stream s in increasing order, all different; the first is 0 and the last is 4095, a one-token document at the stream's end. A document runs from its start to the next start.
All inputs are finite; a program needn't handle non-finite values.
Results may differ from a plain program's by a relative error of at most 0.022.
Values may be sent and summed in bfloat16 or wider, within the bound.
No kernel may reach another device: no remote copies, remote signals or barrier semaphores. Data moves between devices by JAX's collectives and lax.ppermute only.
A program may use at most 192 MiB of HBM per device.

v0:
```python
from functools import partial
import math
import jax
import jax.numpy as jnp
from jax import lax
from jax.sharding import PartitionSpec as P

H = 12
HD = 64
EPSILON = 1e-05
NEGATIVE = -1e30


def layer_norm(resid, gain, shift):
    centre = jnp.mean(resid, axis=-1, keepdims=True)
    centred = resid - centre
    spread = jnp.mean(centred * centred, axis=-1, keepdims=True)
    return centred * lax.rsqrt(spread + EPSILON) * gain + shift


def doc_index(starts, positions):
    return jnp.sum((starts[None, :] <= positions[:, None]).astype(jnp.int32), axis=1) - 1


def over_blocks(block_step, carry, key_rows, value_rows):
    total_rows = key_rows.shape[0]
    size = math.gcd(total_rows, 512)
    count = total_rows // size
    width = key_rows.shape[1]
    key_blocks = key_rows.reshape(count, size, width)
    value_blocks = value_rows.reshape(count, size, width)
    offsets = size * jnp.arange(count, dtype=jnp.int32)

    def inner(state, element):
        offset, key_block, value_block = element
        return (block_step(state, key_block, value_block, offset), None)

    carry, unused = lax.scan(inner, carry, (offsets, key_blocks, value_blocks))
    return carry


def fold_pieces(block_step, carry, piece):
    return over_blocks(block_step, carry, piece[0], piece[1])


def guarded(block_core, starts):

    def wrapped(state, key_block, value_block, offset):
        key_docs = doc_index(starts, offset + jnp.arange(key_block.shape[0], dtype=jnp.int32))
        return block_core(state, key_block, value_block, key_docs, offset)

    return wrapped


def forward_core(query_heads, query_docs, state, key_block, value_block, key_docs, offset):
    best, total, accum = state
    block_len = key_block.shape[0]
    head_count, head_size = (query_heads.shape[1], query_heads.shape[2])
    key_heads = key_block.reshape(block_len, head_count, head_size)
    value_heads = value_block.reshape(block_len, head_count, head_size)
    allowed = (query_docs[:, None] == key_docs[None, :])[None]
    scores = jnp.einsum("qhd,khd->hqk", query_heads, key_heads, preferred_element_type=jnp.float32)
    scores = jnp.where(allowed, scores * head_size ** (-0.5), NEGATIVE)
    new_best = jnp.maximum(best, jnp.max(scores, axis=-1))
    weights = jnp.where(allowed, jnp.exp(scores - new_best[:, :, None]), 0.0)
    shrink = jnp.exp(best - new_best)
    total = total * shrink + jnp.sum(weights, axis=-1)
    update = jnp.einsum(
        "hqk,khd->qhd",
        weights.astype(jnp.bfloat16),
        value_heads,
        preferred_element_type=jnp.float32,
    )
    accum = accum * jnp.transpose(shrink)[:, :, None] + update
    return (new_best, total, accum)


def backward_core(
    query_heads,
    query_docs,
    grad_heads,
    log_total,
    delta,
    state,
    key_block,
    value_block,
    key_docs,
    offset,
):
    grad_query, key_terms = state
    block_len = key_block.shape[0]
    head_count, head_size = (query_heads.shape[1], query_heads.shape[2])
    key_heads = key_block.reshape(block_len, head_count, head_size)
    value_heads = value_block.reshape(block_len, head_count, head_size)
    allowed = (query_docs[:, None] == key_docs[None, :])[None]
    scores = jnp.einsum("qhd,khd->hqk", query_heads, key_heads, preferred_element_type=jnp.float32)
    scores = jnp.where(allowed, scores * head_size ** (-0.5), NEGATIVE)
    probs = jnp.where(allowed, jnp.exp(scores - log_total[:, :, None]), 0.0)
    d_probs = jnp.einsum(
        "qhd,khd->hqk", grad_heads, value_heads, preferred_element_type=jnp.float32
    )
    d_scores = (probs * (d_probs - delta[:, :, None]) * head_size ** (-0.5)).astype(jnp.bfloat16)
    grad_query = grad_query + jnp.einsum(
        "hqk,khd->qhd", d_scores, key_heads, preferred_element_type=jnp.float32
    )
    key_grad = jnp.einsum("hqk,qhd->khd", d_scores, query_heads, preferred_element_type=jnp.float32)
    value_grad = jnp.einsum(
        "hqk,qhd->khd", probs.astype(jnp.bfloat16), grad_heads, preferred_element_type=jnp.float32
    )
    joined = jnp.concatenate(
        [
            key_grad.reshape(block_len, head_count * head_size),
            value_grad.reshape(block_len, head_count * head_size),
        ],
        axis=1,
    )
    key_terms = lax.dynamic_update_slice(key_terms, joined, (offset, 0))
    return (grad_query, key_terms)


def body(
    inputs,
    doc_starts,
    qkv_weight,
    query_bias,
    value_bias,
    out_weight,
    out_bias,
    norm1_gain,
    norm1_bias,
    in_weight,
    in_bias,
    back_weight,
    back_bias,
    norm2_gain,
    norm2_bias,
    cotangent,
):
    (
        qkv_full,
        query_shift,
        value_shift,
        out_full,
        out_shift,
        gain_one,
        shift_one,
        in_full,
        in_shift,
        back_full,
        back_shift,
        gain_two,
        shift_two,
    ) = (
        lax.all_gather(qkv_weight, "fsdp", axis=0, tiled=True),
        lax.all_gather(query_bias, "fsdp", axis=0, tiled=True),
        lax.all_gather(value_bias, "fsdp", axis=0, tiled=True),
        lax.all_gather(out_weight, "fsdp", axis=0, tiled=True),
        lax.all_gather(out_bias, "fsdp", axis=0, tiled=True),
        lax.all_gather(norm1_gain, "fsdp", axis=0, tiled=True),
        lax.all_gather(norm1_bias, "fsdp", axis=0, tiled=True),
        lax.all_gather(in_weight, "fsdp", axis=0, tiled=True),
        lax.all_gather(in_bias, "fsdp", axis=0, tiled=True),
        lax.all_gather(back_weight, "fsdp", axis=0, tiled=True),
        lax.all_gather(back_bias, "fsdp", axis=0, tiled=True),
        lax.all_gather(norm2_gain, "fsdp", axis=0, tiled=True),
        lax.all_gather(norm2_bias, "fsdp", axis=0, tiled=True),
    )
    tokens = inputs[0]
    local_rows = tokens.shape[0]
    model = tokens.shape[1]
    stream_len = local_rows * lax.axis_size("ctx")
    starts = doc_starts[0]
    query_docs = doc_index(
        starts, lax.axis_index("ctx") * local_rows + jnp.arange(local_rows, dtype=jnp.int32)
    )
    projected = jnp.dot(tokens, qkv_full, preferred_element_type=jnp.float32)
    query_low = (projected[:, :model] + query_shift.astype(jnp.float32)).astype(jnp.bfloat16)
    key_low = projected[:, model : 2 * model].astype(jnp.bfloat16)
    value_low = (projected[:, 2 * model :] + value_shift.astype(jnp.float32)).astype(jnp.bfloat16)
    query_heads = query_low.reshape(local_rows, H, HD)
    forward_block = guarded(partial(forward_core, query_heads, query_docs), starts)
    initial = (
        jnp.full((H, local_rows), NEGATIVE, jnp.float32),
        jnp.zeros((H, local_rows), jnp.float32),
        jnp.zeros((local_rows, H, HD), jnp.float32),
    )
    best, total, accum = fold_pieces(
        forward_block,
        initial,
        (
            lax.all_gather(key_low, "ctx", axis=0, tiled=True),
            lax.all_gather(value_low, "ctx", axis=0, tiled=True),
        ),
    )
    log_total = best + jnp.log(total)
    attended = accum / jnp.transpose(total)[:, :, None]
    attended_low = attended.reshape(local_rows, model).astype(jnp.bfloat16)
    branch = jnp.dot(attended_low, out_full, preferred_element_type=jnp.float32) + out_shift.astype(
        jnp.float32
    )
    hidden, norm1_back = jax.vjp(
        layer_norm,
        tokens.astype(jnp.float32) + branch,
        gain_one.astype(jnp.float32),
        shift_one.astype(jnp.float32),
    )
    hidden_low = hidden.astype(jnp.bfloat16)
    pre_act = jnp.dot(hidden_low, in_full, preferred_element_type=jnp.float32) + in_shift.astype(
        jnp.float32
    )
    activated, gelu_back = jax.vjp(partial(jax.nn.gelu, approximate=False), pre_act)
    act_low = activated.astype(jnp.bfloat16)
    ffn_out = jnp.dot(act_low, back_full, preferred_element_type=jnp.float32) + back_shift.astype(
        jnp.float32
    )
    result, norm2_back = jax.vjp(
        layer_norm, hidden + ffn_out, gain_two.astype(jnp.float32), shift_two.astype(jnp.float32)
    )
    d_resid2, grad_gain_two, grad_shift_two = norm2_back(cotangent[0].astype(jnp.float32))
    d_ffn_low = d_resid2.astype(jnp.bfloat16)
    grad_back_full = jnp.einsum("tf,td->fd", act_low, d_ffn_low, preferred_element_type=jnp.float32)
    grad_back_shift = jnp.sum(d_ffn_low, axis=0, dtype=jnp.float32)
    d_act = jnp.einsum("td,fd->tf", d_ffn_low, back_full, preferred_element_type=jnp.float32)
    d_pre_low = gelu_back(d_act)[0].astype(jnp.bfloat16)
    grad_in_full = jnp.einsum(
        "td,tf->df", hidden_low, d_pre_low, preferred_element_type=jnp.float32
    )
    grad_in_shift = jnp.sum(d_pre_low, axis=0, dtype=jnp.float32)
    d_hidden = d_resid2 + jnp.einsum(
        "tf,df->td", d_pre_low, in_full, preferred_element_type=jnp.float32
    )
    d_resid1, grad_gain_one, grad_shift_one = norm1_back(d_hidden)
    d_branch_low = d_resid1.astype(jnp.bfloat16)
    grad_out_full = jnp.einsum(
        "tc,td->cd", attended_low, d_branch_low, preferred_element_type=jnp.float32
    )
    grad_out_shift = jnp.sum(d_branch_low, axis=0, dtype=jnp.float32)
    d_attended_low = jnp.einsum(
        "td,cd->tc", d_branch_low, out_full, preferred_element_type=jnp.float32
    ).astype(jnp.bfloat16)
    grad_heads = d_attended_low.reshape(local_rows, H, HD)
    delta = jnp.transpose(jnp.sum(grad_heads.astype(jnp.float32) * attended, axis=-1))
    backward_block = guarded(
        partial(backward_core, query_heads, query_docs, grad_heads, log_total, delta), starts
    )
    initial_back = (
        jnp.zeros((local_rows, H, HD), jnp.float32),
        jnp.zeros((stream_len, 2 * model), jnp.float32),
    )
    grad_query, key_terms = fold_pieces(
        backward_block,
        initial_back,
        (
            lax.all_gather(key_low, "ctx", axis=0, tiled=True),
            lax.all_gather(value_low, "ctx", axis=0, tiled=True),
        ),
    )
    key_sums = lax.psum_scatter(
        key_terms.astype(jnp.bfloat16), "ctx", scatter_dimension=0, tiled=True
    ).astype(jnp.float32)
    d_query_low = grad_query.reshape(local_rows, model).astype(jnp.bfloat16)
    d_qkv_low = jnp.concatenate(
        [
            d_query_low,
            key_sums[:, :model].astype(jnp.bfloat16),
            key_sums[:, model:].astype(jnp.bfloat16),
        ],
        axis=1,
    )
    grad_qkv_full = jnp.einsum("td,te->de", tokens, d_qkv_low, preferred_element_type=jnp.float32)
    grad_query_shift = jnp.sum(d_query_low, axis=0, dtype=jnp.float32)
    grad_value_shift = jnp.sum(d_qkv_low[:, 2 * model :], axis=0, dtype=jnp.float32)
    input_grad = d_resid1 + jnp.einsum(
        "te,de->td", d_qkv_low, qkv_full, preferred_element_type=jnp.float32
    )
    shards = (
        lax.psum_scatter(
            grad_qkv_full.astype(jnp.bfloat16), "fsdp", scatter_dimension=0, tiled=True
        ).astype(jnp.float32),
        lax.psum_scatter(
            grad_query_shift.astype(jnp.bfloat16), "fsdp", scatter_dimension=0, tiled=True
        ).astype(jnp.float32),
        lax.psum_scatter(
            grad_value_shift.astype(jnp.bfloat16), "fsdp", scatter_dimension=0, tiled=True
        ).astype(jnp.float32),
        lax.psum_scatter(
            grad_out_full.astype(jnp.bfloat16), "fsdp", scatter_dimension=0, tiled=True
        ).astype(jnp.float32),
        lax.psum_scatter(
            grad_out_shift.astype(jnp.bfloat16), "fsdp", scatter_dimension=0, tiled=True
        ).astype(jnp.float32),
        lax.psum_scatter(
            grad_gain_one.astype(jnp.bfloat16), "fsdp", scatter_dimension=0, tiled=True
        ).astype(jnp.float32),
        lax.psum_scatter(
            grad_shift_one.astype(jnp.bfloat16), "fsdp", scatter_dimension=0, tiled=True
        ).astype(jnp.float32),
        lax.psum_scatter(
            grad_in_full.astype(jnp.bfloat16), "fsdp", scatter_dimension=0, tiled=True
        ).astype(jnp.float32),
        lax.psum_scatter(
            grad_in_shift.astype(jnp.bfloat16), "fsdp", scatter_dimension=0, tiled=True
        ).astype(jnp.float32),
        lax.psum_scatter(
            grad_back_full.astype(jnp.bfloat16), "fsdp", scatter_dimension=0, tiled=True
        ).astype(jnp.float32),
        lax.psum_scatter(
            grad_back_shift.astype(jnp.bfloat16), "fsdp", scatter_dimension=0, tiled=True
        ).astype(jnp.float32),
        lax.psum_scatter(
            grad_gain_two.astype(jnp.bfloat16), "fsdp", scatter_dimension=0, tiled=True
        ).astype(jnp.float32),
        lax.psum_scatter(
            grad_shift_two.astype(jnp.bfloat16), "fsdp", scatter_dimension=0, tiled=True
        ).astype(jnp.float32),
    )
    totals = (
        lax.psum(shards[0].astype(jnp.bfloat16), "ctx").astype(jnp.float32),
        lax.psum(shards[1].astype(jnp.bfloat16), "ctx").astype(jnp.float32),
        lax.psum(shards[2].astype(jnp.bfloat16), "ctx").astype(jnp.float32),
        lax.psum(shards[3].astype(jnp.bfloat16), "ctx").astype(jnp.float32),
        lax.psum(shards[4].astype(jnp.bfloat16), "ctx").astype(jnp.float32),
        lax.psum(shards[5].astype(jnp.bfloat16), "ctx").astype(jnp.float32),
        lax.psum(shards[6].astype(jnp.bfloat16), "ctx").astype(jnp.float32),
        lax.psum(shards[7].astype(jnp.bfloat16), "ctx").astype(jnp.float32),
        lax.psum(shards[8].astype(jnp.bfloat16), "ctx").astype(jnp.float32),
        lax.psum(shards[9].astype(jnp.bfloat16), "ctx").astype(jnp.float32),
        lax.psum(shards[10].astype(jnp.bfloat16), "ctx").astype(jnp.float32),
        lax.psum(shards[11].astype(jnp.bfloat16), "ctx").astype(jnp.float32),
        lax.psum(shards[12].astype(jnp.bfloat16), "ctx").astype(jnp.float32),
    )
    return (
        result.astype(jnp.bfloat16)[None],
        input_grad[None],
        totals[0],
        totals[1],
        totals[2],
        totals[3],
        totals[4],
        totals[5],
        totals[6],
        totals[7],
        totals[8],
        totals[9],
        totals[10],
        totals[11],
        totals[12],
    )


def solution(mesh):
    placed = (
        P("fsdp", "ctx", None),
        P("fsdp", None),
        P("fsdp", None),
        P("fsdp"),
        P("fsdp"),
        P("fsdp", None),
        P("fsdp"),
        P("fsdp"),
        P("fsdp"),
        P("fsdp", None),
        P("fsdp"),
        P("fsdp", None),
        P("fsdp"),
        P("fsdp"),
        P("fsdp"),
        P("fsdp", "ctx", None),
    )
    return jax.shard_map(
        body,
        mesh=mesh,
        in_specs=placed,
        out_specs=(
            P("fsdp", "ctx", None),
            P("fsdp", "ctx", None),
            P("fsdp", None),
            P("fsdp"),
            P("fsdp"),
            P("fsdp", None),
            P("fsdp"),
            P("fsdp"),
            P("fsdp"),
            P("fsdp", None),
            P("fsdp"),
            P("fsdp", None),
            P("fsdp"),
            P("fsdp"),
            P("fsdp"),
        ),
        check_vma=False,
    )
```

profile of v0, /device:TPU:0, one launch (start us, length us, event | category | flops | bytes accessed | tf_op | source)
XLA Modules:
  0.0 1406.1 jit_solution(16714513055918829234)
XLA Ops:
  15.8 13.9 all-reduce.20
  29.7 13.5 all-gather.8.cloned.1.call-done
  61.0 88.8 %all-gather.12.cloned.1.call-done = bf16[4096,768]{1,0:T(8,128)(2,1)} async-done(((bf16[512,768]{1,0:T(8,128)(2,1)}), bf16[4096,768]{1,0:T(8,128)(2,1)}) %all-gather.12.cloned.1.call-update) | async-done | bytes 6291472 | tf_op jit(solution)/shard_map/all_gather | solution.py:192
  149.7 8.6 copy.76
  158.3 91.1 %all-gather.10.cloned.1.call-done = bf16[4096,768]{1,0:T(8,128)(2,1)} async-done(((bf16[512,768]{1,0:T(8,128)(2,1)}), bf16[4096,768]{1,0:T(8,128)(2,1)}) %all-gather.10.cloned.1.call-update) | async-done | bytes 6291472 | tf_op jit(solution)/shard_map/all_gather | solution.py:191
  249.4 8.7 copy.75
  258.1 170.9 %while.32 = (s32[]{:T(128)}, f32[12,512]{1,0:T(8,128)S(1)}, f32[12,512]{1,0:T(8,128)S(1)}, f32[512,12,64]{0,2,1:T(8,128)S(1)}, s32[512]{0:T(512)S(1)}, /*index=5...) while((s32[]{:T(128)}, f32[12,512]{1,0:T(8,128)S(1)}, ...), condition=%wide.region_5.6_spmd.clone, body=%wide.region_1.5_spmd.clone.sunk | while | flops 847692288 | bytes 98187464 | solution.py:38
  261.2 6.6 fusion.120
  310.8 7.6 bitcast_add_fusion.4
  326.8 6.6 fusion.120
  333.4 6.6 bitcast_add_fusion.4
  369.0 6.6 fusion.120
  433.5 21.0 %multiply_convert_fusion = (bf16[512,3072]{1,0:T(8,128)(2,1)}, f32[512,3072]{1,0:T(8,128)}, f32[512,3072]{1,0:T(8,128)}) fusion(f32[3072]{0:T(1024)S(1)} %bitcast.195, bf16[768,3072]{1,0:T(8,128)(2,1)} %all-gather.16.cloned.1.call-done, f32[512,768]{1,0:T(8,128)} %copy-done.12, f32[768]{0:T(1024)S(1)} %convert_element_type.229, ...), kind=kOutput, calls=%fused_computation.47 | convolution fusion | flops 2521694208 | bytes 22042624 | tf_op jit(solution)/shard_map/dot_general | solution.py:208
  465.1 8.7 fusion.53
  490.6 366.8 %while.33 = (s32[]{:T(128)}, f32[512,12,64]{0,2,1:T(8,128)}, bf16[4096,1536]{0,1:T(8,128)(2,1)}, bf16[8,512,768]{1,2,0:T(8,128)(2,1)}, s32[512]{0:T(512)S(1)}, /...) while((s32[]{:T(128)}, f32[512,12,64]{0,2,1:T(8,128)}, ...), condition=%wide.region_17.18_spmd.clone, body=%wide.region_15.17_spmd.clone.sunk | while | flops 2058367488 | bytes 114907512 | solution.py:38
  516.8 14.6 %dynamic_update_slice.8 = bf16[4096,1536]{0,1:T(8,128)(2,1)} dynamic-update-slice(bf16[4096,1536]{0,1:T(8,128)(2,1)} %get-tuple-element.831, bf16[512,1536]{0,1:T(8,128)(2,1)S(1)} %pad_maximum_fusion.7, s32[]{:T(128)S(6)} %select_n.93, s32[]{:T(128)} %constant.145.clone.1..sunk.1) | dynamic-update-slice | bytes 3145732 | tf_op jit(solution)/shard_map/while/body/eval_jaxpr/dynamic_update_slice | solution.py:117
  562.4 14.7 %dynamic_update_slice.8 = bf16[4096,1536]{0,1:T(8,128)(2,1)} dynamic-update-slice(bf16[4096,1536]{0,1:T(8,128)(2,1)} %get-tuple-element.831, bf16[512,1536]{0,1:T(8,128)(2,1)S(1)} %pad_maximum_fusion.7, s32[]{:T(128)S(6)} %select_n.93, s32[]{:T(128)} %constant.145.clone.1..sunk.1) | dynamic-update-slice | bytes 3145732 | tf_op jit(solution)/shard_map/while/body/eval_jaxpr/dynamic_update_slice | solution.py:117
  608.3 14.7 %dynamic_update_slice.8 = bf16[4096,1536]{0,1:T(8,128)(2,1)} dynamic-update-slice(bf16[4096,1536]{0,1:T(8,128)(2,1)} %get-tuple-element.831, bf16[512,1536]{0,1:T(8,128)(2,1)S(1)} %pad_maximum_fusion.7, s32[]{:T(128)S(6)} %select_n.93, s32[]{:T(128)} %constant.145.clone.1..sunk.1) | dynamic-update-slice | bytes 3145732 | tf_op jit(solution)/shard_map/while/body/eval_jaxpr/dynamic_update_slice | solution.py:117
  654.4 14.7 %dynamic_update_slice.8 = bf16[4096,1536]{0,1:T(8,128)(2,1)} dynamic-update-slice(bf16[4096,1536]{0,1:T(8,128)(2,1)} %get-tuple-element.831, bf16[512,1536]{0,1:T(8,128)(2,1)S(1)} %pad_maximum_fusion.7, s32[]{:T(128)S(6)} %select_n.93, s32[]{:T(128)} %constant.145.clone.1..sunk.1) | dynamic-update-slice | bytes 3145732 | tf_op jit(solution)/shard_map/while/body/eval_jaxpr/dynamic_update_slice | solution.py:117
  700.4 14.7 %dynamic_update_slice.8 = bf16[4096,1536]{0,1:T(8,128)(2,1)} dynamic-update-slice(bf16[4096,1536]{0,1:T(8,128)(2,1)} %get-tuple-element.831, bf16[512,1536]{0,1:T(8,128)(2,1)S(1)} %pad_maximum_fusion.7, s32[]{:T(128)S(6)} %select_n.93, s32[]{:T(128)} %constant.145.clone.1..sunk.1) | dynamic-update-slice | bytes 3145732 | tf_op jit(solution)/shard_map/while/body/eval_jaxpr/dynamic_update_slice | solution.py:117
  746.5 14.6 %dynamic_update_slice.8 = bf16[4096,1536]{0,1:T(8,128)(2,1)} dynamic-update-slice(bf16[4096,1536]{0,1:T(8,128)(2,1)} %get-tuple-element.831, bf16[512,1536]{0,1:T(8,128)(2,1)S(1)} %pad_maximum_fusion.7, s32[]{:T(128)S(6)} %select_n.93, s32[]{:T(128)} %constant.145.clone.1..sunk.1) | dynamic-update-slice | bytes 3145732 | tf_op jit(solution)/shard_map/while/body/eval_jaxpr/dynamic_update_slice | solution.py:117
  792.4 14.6 %dynamic_update_slice.8 = bf16[4096,1536]{0,1:T(8,128)(2,1)} dynamic-update-slice(bf16[4096,1536]{0,1:T(8,128)(2,1)} %get-tuple-element.831, bf16[512,1536]{0,1:T(8,128)(2,1)S(1)} %pad_maximum_fusion.7, s32[]{:T(128)S(6)} %select_n.93, s32[]{:T(128)} %constant.145.clone.1..sunk.1) | dynamic-update-slice | bytes 3145732 | tf_op jit(solution)/shard_map/while/body/eval_jaxpr/dynamic_update_slice | solution.py:117
  838.4 13.5 dynamic_update_slice.8
  859.8 203.3 %reduce-scatter.8.cloned.1.call-done = bf16[512,1536]{0,1:T(8,128)(2,1)} async-done(((bf16[4096,1536]{0,1:T(8,128)(2,1)}), bf16[512,1536]{0,1:T(8,128)(2,1)}) %reduce-scatter.8.cloned.1.call-update) | async-done | bytes 1572880 | tf_op jit(solution)/shard_map/reduce_scatter | solution.py:258
  1074.5 7.3 convolution_convert_fusion
  1089.9 20.8 %reduce-scatter.16.cloned.1.call-done = bf16[192,2304]{1,0:T(8,128)(2,1)} async-done(((bf16[768,2304]{1,0:T(8,128)(2,1)}), bf16[192,2304]{1,0:T(8,128)(2,1)}) %reduce-scatter.16.cloned.1.call-update) | async-done | bytes 884752
  1113.0 25.9 %reduce-scatter.10.cloned.1.call-done = bf16[192,768]{1,0:T(8,128)(2,1)} async-done(((bf16[768,768]{1,0:T(8,128)(2,1)}), bf16[192,768]{1,0:T(8,128)(2,1)}) %reduce-scatter.10.cloned.1.call-update) | async-done | bytes 294928 | tf_op jit(solution)/shard_map/reduce_scatter | solution.py:286
  1138.9 50.4 %reduce-scatter.14.cloned.1.call-done = bf16[768,768]{1,0:T(8,128)(2,1)} async-done(((bf16[3072,768]{1,0:T(8,128)(2,1)}), bf16[768,768]{1,0:T(8,128)(2,1)}) %reduce-scatter.14.cloned.1.call-update) | async-done | bytes 1179664 | tf_op jit(solution)/shard_map/reduce_scatter | solution.py:304
  1189.3 50.5 %reduce-scatter.12.cloned.1.call-done = bf16[192,3072]{1,0:T(8,128)(2,1)} async-done(((bf16[768,3072]{1,0:T(8,128)(2,1)}), bf16[192,3072]{1,0:T(8,128)(2,1)}) %reduce-scatter.12.cloned.1.call-update) | async-done | bytes 1179664 | tf_op jit(solution)/shard_map/reduce_scatter | solution.py:298
  1243.1 10.3 all-reduce.19
  1254.0 23.2 %all-reduce.17 = (bf16[192]{0:T(256)(128)(2,1)S(1)}, bf16[192]{0:T(256)(128)(2,1)S(1)}, bf16[192]{0:T(256)(128)(2,1)S(1)}, bf16[192]{0:T(256)(128)(2,1)S(1)}, bf...) all-reduce(bf16[192]{0:T(256)(128)(2,1)S(1)} %dynamic-slice.9, ...), channel_id=1, replica_groups=mesh['ctx'=8,'fsdp'=4] {'ctx'}, use_global_device_ids=true, to_apply=%region_23.24 | all-reduce | flops 2304 | bytes 9216 | tf_op jit(solution)/shard_map/psum | solution.py:319
  1289.8 102.2 %all-reduce.23.cloned.1.call-done = (bf16[192,2304]{0,1:T(8,128)(2,1)}, bf16[192,768]{1,0:T(8,128)(2,1)}, bf16[192,3072]{1,0:T(8,128)(2,1)}, bf16[768,768]{1,0:T(8,128)(2,1)}) async-done(((bf16[192,2304]{0,1:T(8,128)(2,1)}, bf16[192,768]{1,0:T(8,128)(2,1)}, bf16[192,3072]{1,0:T(8,128)(2,1)}, bf16[768,768]{1,0:T(8,128)(2,1)}), (bf16[192,2304]{0,1:T(8,128)(2,1)}, bf16[192,768]{1,0:T(8,128)(2,1)}, ...) | async-done | bytes 3538960 | tf_op jit(solution)/shard_map/psum | solution.py:318
  (508 shorter events, 473.6 us)
Async XLA Ops:
  7.2 36.0 %all-gather.8.cloned.1.call-start = ((), (), s32[]{:S(2)}) async-start(), calls=%async_computation.5 | async-start | bytes 4423680 | tf_op jit(solution)/shard_map/all_gather | solution.py:154
  7.9 141.8 %all-gather.12.cloned.1.call-start = ((), (), s32[]{:S(2)}) async-start(), calls=%async_computation.7 | async-start | bytes 7077888 | tf_op jit(solution)/shard_map/all_gather | solution.py:192
  50.8 198.6 %all-gather.10.cloned.1.call-start = ((), (), s32[]{:S(2)}) async-start(), calls=%async_computation.6 | async-start | bytes 7077888 | tf_op jit(solution)/shard_map/all_gather | solution.py:191
  53.3 376.0 %all-gather.14.cloned.1.call-start = ((), (), s32[]{:S(2)}) async-start(), calls=%async_computation.8 | async-start | bytes 1474560 | tf_op jit(solution)/shard_map/all_gather | solution.py:157
  53.8 379.6 %all-gather.16.cloned.1.call-start = ((), (), s32[]{:S(2)}) async-start(), calls=%async_computation.9 | async-start | bytes 5898240 | tf_op jit(solution)/shard_map/all_gather | solution.py:161
  54.4 400.1 %all-gather.18.cloned.1.call-start = ((), (), s32[]{:S(2)}) async-start(), calls=%async_computation.10 | async-start | bytes 5898240 | tf_op jit(solution)/shard_map/all_gather | solution.py:163
  55.0 1008.1 %reduce-scatter.8.cloned.1.call-start = ((), (), s32[]{:S(2)}) async-start(), calls=%async_computation.11 | async-start | bytes 14155776 | tf_op jit(solution)/shard_map/reduce_scatter | solution.py:258
  55.2 422.3 %copy-start.35 = (f32[768]{0:T(1024)}, f32[768]{0:T(1024)S(1)}, u32[]{:S(2)}) copy-start(f32[768]{0:T(1024)S(1)} %convert_element_type.228) | copy-start | bytes 9220
  55.3 399.3 %copy-start.45 = (f32[768]{0:T(1024)}, f32[768]{0:T(1024)S(1)}, u32[]{:S(2)}) copy-start(f32[768]{0:T(1024)S(1)} %convert_element_type.229) | copy-start | bytes 9220
  60.7 402.1 %copy-start.26 = (f32[768]{0:T(1024)}, f32[768]{0:T(1024)S(1)}, u32[]{:S(2)}) copy-start(f32[768]{0:T(1024)S(1)} %convert_element_type.234) | copy-start | bytes 9220
  429.2 25.2 %copy-start.18 = (bf16[512,12,64]{0,2,1:T(8,128)(2,1)}, bf16[512,12,64]{0,2,1:T(8,128)(2,1)S(1)}, u32[]{:S(2)}) copy-start(bf16[512,12,64]{0,2,1:T(8,128)(2,1)S(1)} %fusion.44) | copy-start | bytes 2359300
  432.0 45.6 %copy-start.33 = (f32[512]{0:T(512)}, f32[512]{0:T(512)S(1)}, u32[]{:S(2)}) copy-start(f32[512]{0:T(512)S(1)} %broadcast_multiply_fusion.1) | copy-start | bytes 6148
  433.4 44.1 %copy-start.42 = (f32[512]{0:T(512)}, f32[512]{0:T(512)S(1)}, u32[]{:S(2)}) copy-start(f32[512]{0:T(512)S(1)} %fusion.45) | copy-start | bytes 6148
  857.4 253.3 %reduce-scatter.16.cloned.1.call-start = ((), (), s32[]{:S(2)}) async-start(), calls=%async_computation.15 | async-start | bytes 4423680
  1071.1 67.9 %reduce-scatter.10.cloned.1.call-start = ((), (), s32[]{:S(2)}) async-start(), calls=%async_computation.12 | async-start | bytes 1474560 | tf_op jit(solution)/shard_map/reduce_scatter | solution.py:286
  1074.2 115.1 %reduce-scatter.14.cloned.1.call-start = ((), (), s32[]{:S(2)}) async-start(), calls=%async_computation.14 | async-start | bytes 5898240 | tf_op jit(solution)/shard_map/reduce_scatter | solution.py:304
  1081.8 158.1 %reduce-scatter.12.cloned.1.call-start = ((), (), s32[]{:S(2)}) async-start(), calls=%async_computation.13 | async-start | bytes 5898240 | tf_op jit(solution)/shard_map/reduce_scatter | solution.py:298
  1089.7 150.2 %copy-start.10 = (bf16[1,512,768]{2,1,0:T(8,128)(2,1)S(1)}, bf16[1,512,768]{2,1,0:T(8,128)(2,1)}, u32[]{:S(2)}) copy-start(bf16[1,512,768]{2,1,0:T(8,128)(2,1)} %param.35) | copy-start | bytes 2359300
  1089.7 151.7 %copy-start.52 = (bf16[192]{0:T(256)(128)(2,1)S(1)}, bf16[192]{0:T(256)(128)(2,1)}, u32[]{:S(2)}) copy-start(bf16[192]{0:T(256)(128)(2,1)} %param.34) | copy-start | bytes 1156
  1089.7 153.3 %copy-start.37 = (bf16[768]{0:T(1024)(128)(2,1)S(1)}, bf16[768]{0:T(1024)(128)(2,1)}, u32[]{:S(2)}) copy-start(bf16[768]{0:T(1024)(128)(2,1)} %get-tuple-element.519) | copy-start | bytes 4612
  1089.7 153.3 %copy-start.38 = (bf16[768]{0:T(1024)(128)(2,1)S(1)}, bf16[768]{0:T(1024)(128)(2,1)}, u32[]{:S(2)}) copy-start(bf16[768]{0:T(1024)(128)(2,1)} %get-tuple-element.598) | copy-start | bytes 4612
  1089.7 153.3 %copy-start.39 = (bf16[768]{0:T(1024)(128)(2,1)S(1)}, bf16[768]{0:T(1024)(128)(2,1)}, u32[]{:S(2)}) copy-start(bf16[768]{0:T(1024)(128)(2,1)} %get-tuple-element.602) | copy-start | bytes 4612
  1089.8 153.3 %copy-start.44 = (bf16[3072]{0:T(1024)(128)(2,1)S(1)}, bf16[3072]{0:T(1024)(128)(2,1)}, u32[]{:S(2)}) copy-start(bf16[3072]{0:T(1024)(128)(2,1)} %get-tuple-element.600) | copy-start | bytes 18436
  1089.8 153.3 %copy-start.47 = (bf16[768]{0:T(1024)(128)(2,1)S(1)}, bf16[768]{0:T(1024)(128)(2,1)}, u32[]{:S(2)}) copy-start(bf16[768]{0:T(1024)(128)(2,1)} %get-tuple-element.517) | copy-start | bytes 4612
  1089.8 153.3 %copy-start.48 = (bf16[768]{0:T(1024)(128)(2,1)S(1)}, bf16[768]{0:T(1024)(128)(2,1)}, u32[]{:S(2)}) copy-start(bf16[768]{0:T(1024)(128)(2,1)} %get-tuple-element.521) | copy-start | bytes 4612
  1089.8 192.6 %copy-start.8 = (f32[512,768]{1,0:T(8,128)S(1)}, f32[512,768]{1,0:T(8,128)}, u32[]{:S(2)}) copy-start(f32[512,768]{1,0:T(8,128)} %copy-done.7) | copy-start | bytes 4718596
  1089.8 192.6 %copy-start.27 = (f32[768]{0:T(1024)S(1)}, f32[768]{0:T(1024)}, u32[]{:S(2)}) copy-start(f32[768]{0:T(1024)} %copy-done.26) | copy-start | bytes 9220
  1089.8 192.6 %copy-start.30 = (f32[512]{0:T(512)S(1)}, f32[512]{0:T(512)}, u32[]{:S(2)}) copy-start(f32[512]{0:T(512)} %copy-done.29) | copy-start | bytes 6148
  1089.8 192.6 %copy-start.32 = (f32[512]{0:T(512)S(1)}, f32[512]{0:T(512)}, u32[]{:S(2)}) copy-start(f32[512]{0:T(512)} %copy-done.31) | copy-start | bytes 6148
  1089.8 302.2 %all-reduce.23.cloned.1.call-start = ((), (), s32[]{:S(2)}) async-start(), calls=%async_computation.16 | async-start | bytes 7667712 | tf_op jit(solution)/shard_map/psum | solution.py:318
  1239.8 43.8 %copy-start.20 = (bf16[512,12,64]{0,2,1:T(8,128)(2,1)S(1)}, bf16[512,12,64]{0,2,1:T(8,128)(2,1)}, u32[]{:S(2)}) copy-start(bf16[512,12,64]{0,2,1:T(8,128)(2,1)} %get-tuple-element.605) | copy-start | bytes 2359300
  1239.9 43.8 %copy-start.41 = (f32[512]{0:T(512)S(1)}, f32[512]{0:T(512)}, u32[]{:S(2)}) copy-start(f32[512]{0:T(512)} %copy-done.40) | copy-start | bytes 6148
  (78 other events, 439.0 us)
Sparse Core Ops, SparseCore 0:
  9.5 33.6 all-gather.7
  50.9 98.7 all-gather.11
  152.5 96.8 all-gather.9
  250.8 15.6 all-gather.13
  267.9 37.4 all-gather.15
  306.8 37.4 all-gather.17
  857.5 205.5 reduce-scatter.7
  1071.2 39.4 reduce-scatter.15
  1113.3 25.6 reduce-scatter.9
  1141.3 47.9 reduce-scatter.13
  1191.8 47.9 reduce-scatter.11
  1244.3 147.7 all-reduce.22
where the time goes:
time: 1420 us; the launch traced here: 1410 us
  waiting for transfers between devices  649 us (46%)
  matrix products  374 us (26%)
  local copies, waits for them, and re-layouts  220 us (15%)
  other arithmetic  75.2 us (5%)
  blocking collectives  52.7 us (4%)
  loops' own time  17.1 us (1%)
  between operations  17.1 us (1%)
    reduce_scatter x1, waiting for transfers between devices, body(): lax.psum_scatter(key_terms.astype(jnp.bfloat16), 'ctx', scatter_dimension...  203 us
    dynamic_update_slice x8, local copies, waits for them, and re-layouts, backward_core(): key_terms = lax.dynamic_update_slice(key_terms, joined, (offset, 0))  116 us
    psum x1, waiting for transfers between devices, body(): lax.psum(shards[0].astype(jnp.bfloat16), 'ctx').astype(jnp.float32)  102 us
    all_gather x1, waiting for transfers between devices, body(): lax.all_gather(key_low, 'ctx', axis=0, tiled=True)  91.1 us
    all_gather x1, waiting for transfers between devices, body(): lax.all_gather(value_low, 'ctx', axis=0, tiled=True)  88.8 us
    dot_general x8, matrix products, forward_core(): jnp.einsum('hqk,khd->qhd', weights.astype(jnp.bfloat16), value_heads, pre...  53.2 us
    dot_general x8, matrix products, forward_core(): jnp.einsum('qhd,khd->hqk', query_heads, key_heads, preferred_element_type...  52.6 us
    reduce_scatter x1, waiting for transfers between devices, body(): lax.psum_scatter(grad_in_full.astype(jnp.bfloat16), 'fsdp', scatter_dimen...  50.5 us
  transfers between devices with their start and end apart: 12, of which 9 were waited for; matrix products, arithmetic and copies ran while one was open for 17% of the time, Pallas kernels for 0%

commit v1 on v0

--- a/solution.py
+++ b/solution.py
@@ -315,7 +315,7 @@
         ).astype(jnp.float32),
     )
     totals = (
-        lax.psum(shards[0].astype(jnp.bfloat16), "ctx").astype(jnp.float32),
+        jnp.sum(lax.all_gather(shards[0].astype(jnp.bfloat16), "ctx"), axis=0).astype(jnp.float32),
         lax.psum(shards[1].astype(jnp.bfloat16), "ctx").astype(jnp.float32),
         lax.psum(shards[2].astype(jnp.bfloat16), "ctx").astype(jnp.float32),
         lax.psum(shards[3].astype(jnp.bfloat16), "ctx").astype(jnp.float32),

time: 1420 us -> 1490 us (1.049)
  waiting for transfers between devices: 649 us -> 721 us
    all_gather x0 -> x1, waiting for transfers between devices: none -> 57.7 us  [body(): lax.all_gather(shards[0].astype(jnp.bfloat16), 'ctx')]
    reduce_scatter x0 -> x1, waiting for transfers between devices: none -> 42.9 us  [body(): lax.psum_scatter(grad_qkv_full.astype(jnp.bfloat16), 'fsdp', scatter_dime...]
    unnamed x13, waiting for transfers between devices: 23.2 us -> 2.41 us
    reduce_scatter x1, waiting for transfers between devices: 203 us -> 185 us  [body(): lax.psum_scatter(key_terms.astype(jnp.bfloat16), 'ctx', scatter_dimension...]
    psum x1, waiting for transfers between devices: 102 us -> 118 us  [body(): lax.psum(shards[3].astype(jnp.bfloat16), 'ctx').astype(jnp.float32)]
    unnamed x132 -> x130, local copies, waits for them, and re-layouts: 43.5 us -> 39.6 us
  transfers between devices with their start and end apart: 12 -> 13, of which waited for: 9 -> 10; matrix products, arithmetic and copies ran while one was open for 17% -> 17% of each run, Pallas kernels for 0% -> 0%
where the time goes in v1:
time: 1490 us; the launch traced here: 1480 us
  waiting for transfers between devices  721 us (48%)
  matrix products  374 us (25%)
  local copies, waits for them, and re-layouts  216 us (14%)
  other arithmetic  79.8 us (5%)
  blocking collectives  52.2 us (4%)
  loops' own time  17.1 us (1%)
  between operations  16.8 us (1%)
    reduce_scatter x1, waiting for transfers between devices, body(): lax.psum_scatter(key_terms.astype(jnp.bfloat16), 'ctx', scatter_dimension...  185 us
    psum x1, waiting for transfers between devices, body(): lax.psum(shards[3].astype(jnp.bfloat16), 'ctx').astype(jnp.float32)  118 us
    dynamic_update_slice x8, local copies, waits for them, and re-layouts, backward_core(): key_terms = lax.dynamic_update_slice(key_terms, joined, (offset, 0))  116 us
    all_gather x1, waiting for transfers between devices, body(): lax.all_gather(key_low, 'ctx', axis=0, tiled=True)  91.1 us
    all_gather x1, waiting for transfers between devices, body(): lax.all_gather(value_low, 'ctx', axis=0, tiled=True)  88.8 us
    all_gather x1, waiting for transfers between devices, body(): lax.all_gather(shards[0].astype(jnp.bfloat16), 'ctx')  57.7 us
    dot_general x8, matrix products, forward_core(): jnp.einsum('hqk,khd->qhd', weights.astype(jnp.bfloat16), value_heads, pre...  53.2 us
    dot_general x8, matrix products, forward_core(): jnp.einsum('qhd,khd->hqk', query_heads, key_heads, preferred_element_type...  52.6 us
  transfers between devices with their start and end apart: 13, of which 10 were waited for; matrix products, arithmetic and copies ran while one was open for 17% of the time, Pallas kernels for 0%

profile of v1, /device:TPU:0, one launch (start us, length us, event | category | flops | bytes accessed | tf_op | source)
XLA Modules:
  0.0 1477.7 jit_solution(13727942647578431675)
XLA Ops:
  15.8 13.9 all-reduce.20
  29.7 13.5 all-gather.10.cloned.1.call-done
  61.0 88.8 %all-gather.14.cloned.1.call-done = bf16[4096,768]{1,0:T(8,128)(2,1)} async-done(((bf16[512,768]{1,0:T(8,128)(2,1)}), bf16[4096,768]{1,0:T(8,128)(2,1)}) %all-gather.14.cloned.1.call-update) | async-done | bytes 6291472 | tf_op jit(solution)/shard_map/all_gather | solution.py:192
  149.7 8.6 copy.75
  158.3 91.1 %all-gather.12.cloned.1.call-done = bf16[4096,768]{1,0:T(8,128)(2,1)} async-done(((bf16[512,768]{1,0:T(8,128)(2,1)}), bf16[4096,768]{1,0:T(8,128)(2,1)}) %all-gather.12.cloned.1.call-update) | async-done | bytes 6291472 | tf_op jit(solution)/shard_map/all_gather | solution.py:191
  249.4 8.7 copy.74
  258.1 170.9 %while.32 = (s32[]{:T(128)}, f32[12,512]{1,0:T(8,128)S(1)}, f32[12,512]{1,0:T(8,128)S(1)}, f32[512,12,64]{0,2,1:T(8,128)S(1)}, s32[512]{0:T(512)S(1)}, /*index=5...) while((s32[]{:T(128)}, f32[12,512]{1,0:T(8,128)S(1)}, ...), condition=%wide.region_5.6_spmd.clone, body=%wide.region_1.5_spmd.clone.sunk | while | flops 847692288 | bytes 98187464 | solution.py:38
  310.8 7.6 bitcast_add_fusion.4
  333.4 6.6 bitcast_add_fusion.4
  433.5 21.0 %multiply_convert_fusion = (bf16[512,3072]{1,0:T(8,128)(2,1)}, f32[512,3072]{1,0:T(8,128)}, f32[512,3072]{1,0:T(8,128)}) fusion(f32[3072]{0:T(1024)S(1)} %bitcast.197, bf16[768,3072]{1,0:T(8,128)(2,1)} %all-gather.18.cloned.1.call-done, f32[512,768]{1,0:T(8,128)} %copy-done.13, f32[768]{0:T(1024)S(1)} %convert_element_type.231, ...), kind=kOutput, calls=%fused_computation.47 | convolution fusion | flops 2521694208 | bytes 22042624 | tf_op jit(solution)/shard_map/dot_general | solution.py:208
  465.1 8.7 fusion.53
  490.7 366.6 %while.33 = (s32[]{:T(128)}, f32[512,12,64]{0,2,1:T(8,128)}, bf16[4096,1536]{0,1:T(8,128)(2,1)}, bf16[8,512,768]{1,2,0:T(8,128)(2,1)}, s32[512]{0:T(512)S(1)}, /...) while((s32[]{:T(128)}, f32[512,12,64]{0,2,1:T(8,128)}, ...), condition=%wide.region_17.18_spmd.clone, body=%wide.region_15.17_spmd.clone.sunk | while | flops 2058367488 | bytes 114907512 | solution.py:38
  516.8 14.6 dynamic_update_slice.8
  562.3 14.7 dynamic_update_slice.8
  608.3 14.7 dynamic_update_slice.8
  654.3 14.7 dynamic_update_slice.8
  700.4 14.7 dynamic_update_slice.8
  746.3 14.6 dynamic_update_slice.8
  792.3 14.6 dynamic_update_slice.8
  838.2 13.5 dynamic_update_slice.8
  860.5 6.8 convolution_convert_fusion
  868.7 6.7 convolution_convert_fusion.1
  877.8 185.1 %reduce-scatter.8.cloned.1.call-done = bf16[512,1536]{0,1:T(8,128)(2,1)} async-done(((bf16[4096,1536]{0,1:T(8,128)(2,1)}), bf16[512,1536]{0,1:T(8,128)(2,1)}) %reduce-scatter.8.cloned.1.call-update) | async-done | bytes 1572880 | tf_op jit(solution)/shard_map/reduce_scatter | solution.py:258
  1070.9 20.0 %reduce-scatter.10.cloned.1.call-done = bf16[192,768]{1,0:T(8,128)(2,1)} async-done(((bf16[768,768]{1,0:T(8,128)(2,1)}), bf16[192,768]{1,0:T(8,128)(2,1)}) %reduce-scatter.10.cloned.1.call-update) | async-done | bytes 294928 | tf_op jit(solution)/shard_map/reduce_scatter | solution.py:286
  1090.8 50.6 %reduce-scatter.14.cloned.1.call-done = bf16[768,768]{1,0:T(8,128)(2,1)} async-done(((bf16[3072,768]{1,0:T(8,128)(2,1)}), bf16[768,768]{1,0:T(8,128)(2,1)}) %reduce-scatter.14.cloned.1.call-update) | async-done | bytes 1179664 | tf_op jit(solution)/shard_map/reduce_scatter | solution.py:304
  1141.4 50.4 %reduce-scatter.12.cloned.1.call-done = bf16[192,3072]{1,0:T(8,128)(2,1)} async-done(((bf16[768,3072]{1,0:T(8,128)(2,1)}), bf16[192,3072]{1,0:T(8,128)(2,1)}) %reduce-scatter.12.cloned.1.call-update) | async-done | bytes 1179664 | tf_op jit(solution)/shard_map/reduce_scatter | solution.py:298
  1191.9 42.9 %reduce-scatter.16.cloned.1.call-done = bf16[192,2304]{1,0:T(8,128)(2,1)} async-done(((bf16[768,2304]{1,0:T(8,128)(2,1)}), bf16[192,2304]{1,0:T(8,128)(2,1)}) %reduce-scatter.16.cloned.1.call-update) | async-done | bytes 884752 | tf_op jit(solution)/shard_map/reduce_scatter | solution.py:277
  1236.6 118.5 %all-reduce.23.cloned.1.call-done = (bf16[192,768]{1,0:T(8,128)(2,1)}, bf16[192,3072]{1,0:T(8,128)(2,1)}, bf16[768,768]{1,0:T(8,128)(2,1)}) async-done(((bf16[192,768]{1,0:T(8,128)(2,1)}, bf16[192,3072]{1,0:T(8,128)(2,1)}, bf16[768,768]{1,0:T(8,128)(2,1)}), (bf16[192,768]{1,0:T(8,128)(2,1)}, bf16[192,3072]{1,0:T(8,128)(2,1)}, bf16[768,768]{1,0:T(8,128)(2,1)})) %all-reduce.23.cloned.1.call-update) | async-done | bytes 2654224 | tf_op jit(solution)/shard_map/psum | solution.py:321
  1360.9 10.7 all-reduce.19
  1372.3 22.3 %all-reduce.17 = (bf16[192]{0:T(256)(128)(2,1)S(1)}, bf16[192]{0:T(256)(128)(2,1)S(1)}, bf16[192]{0:T(256)(128)(2,1)S(1)}, bf16[192]{0:T(256)(128)(2,1)S(1)}, bf...) all-reduce(bf16[192]{0:T(256)(128)(2,1)S(1)} %dynamic-slice.9, ...), channel_id=1, replica_groups=mesh['ctx'=8,'fsdp'=4] {'ctx'}, use_global_device_ids=true, to_apply=%region_23.24 | all-reduce | flops 2304 | bytes 9216 | tf_op jit(solution)/shard_map/psum | solution.py:319
  1400.9 6.6 add_bitcast_fusion
  1407.5 57.7 %all-gather.22.cloned.1.call-done = bf16[1536,2304]{1,0:T(8,128)(2,1)} async-done(((bf16[192,2304]{1,0:T(8,128)(2,1)}), bf16[1536,2304]{1,0:T(8,128)(2,1)}) %all-gather.22.cloned.1.call-update) | async-done | bytes 7077904 | tf_op jit(solution)/shard_map/all_gather | solution.py:318
  (511 shorter events, 481.0 us)
Async XLA Ops:
  7.2 36.0 %all-gather.10.cloned.1.call-start = ((), (), s32[]{:S(2)}) async-start(), calls=%async_computation.5 | async-start | bytes 4423680 | tf_op jit(solution)/shard_map/all_gather | solution.py:154
  7.9 141.8 %all-gather.14.cloned.1.call-start = ((), (), s32[]{:S(2)}) async-start(), calls=%async_computation.7 | async-start | bytes 7077888 | tf_op jit(solution)/shard_map/all_gather | solution.py:192
  50.8 198.6 %all-gather.12.cloned.1.call-start = ((), (), s32[]{:S(2)}) async-start(), calls=%async_computation.6 | async-start | bytes 7077888 | tf_op jit(solution)/shard_map/all_gather | solution.py:191
  53.3 376.0 %all-gather.16.cloned.1.call-start = ((), (), s32[]{:S(2)}) async-start(), calls=%async_computation.8 | async-start | bytes 1474560 | tf_op jit(solution)/shard_map/all_gather | solution.py:157
  53.8 379.6 %all-gather.18.cloned.1.call-start = ((), (), s32[]{:S(2)}) async-start(), calls=%async_computation.9 | async-start | bytes 5898240 | tf_op jit(solution)/shard_map/all_gather | solution.py:161
  54.4 400.1 %all-gather.20.cloned.1.call-start = ((), (), s32[]{:S(2)}) async-start(), calls=%async_computation.10 | async-start | bytes 5898240 | tf_op jit(solution)/shard_map/all_gather | solution.py:163
  55.0 1008.0 %reduce-scatter.8.cloned.1.call-start = ((), (), s32[]{:S(2)}) async-start(), calls=%async_computation.11 | async-start | bytes 14155776 | tf_op jit(solution)/shard_map/reduce_scatter | solution.py:258
  55.2 422.3 %copy-start.35 = (f32[768]{0:T(1024)}, f32[768]{0:T(1024)S(1)}, u32[]{:S(2)}) copy-start(f32[768]{0:T(1024)S(1)} %convert_element_type.230) | copy-start | bytes 9220
  55.3 399.3 %copy-start.45 = (f32[768]{0:T(1024)}, f32[768]{0:T(1024)S(1)}, u32[]{:S(2)}) copy-start(f32[768]{0:T(1024)S(1)} %convert_element_type.231) | copy-start | bytes 9220
  60.7 402.1 %copy-start.26 = (f32[768]{0:T(1024)}, f32[768]{0:T(1024)S(1)}, u32[]{:S(2)}) copy-start(f32[768]{0:T(1024)S(1)} %convert_element_type.236) | copy-start | bytes 9220
  429.2 25.2 %copy-start.18 = (bf16[512,12,64]{0,2,1:T(8,128)(2,1)}, bf16[512,12,64]{0,2,1:T(8,128)(2,1)S(1)}, u32[]{:S(2)}) copy-start(bf16[512,12,64]{0,2,1:T(8,128)(2,1)S(1)} %fusion.44) | copy-start | bytes 2359300
  432.0 45.6 %copy-start.33 = (f32[512]{0:T(512)}, f32[512]{0:T(512)S(1)}, u32[]{:S(2)}) copy-start(f32[512]{0:T(512)S(1)} %broadcast_multiply_fusion.1) | copy-start | bytes 6148
  433.4 44.1 %copy-start.42 = (f32[512]{0:T(512)}, f32[512]{0:T(512)S(1)}, u32[]{:S(2)}) copy-start(f32[512]{0:T(512)S(1)} %fusion.45) | copy-start | bytes 6148
  558.8 18.1 %copy-start.5 = (bf16[1,512,768]{1,2,0:T(8,128)(2,1)S(1)}, bf16[1,512,768]{1,2,0:T(8,128)(2,1)}, u32[]{:S(2)}) copy-start(bf16[1,512,768]{1,2,0:T(8,128)(2,1)} %copy-done.4) | copy-start | bytes 2359300 | tf_op jit(solution)/shard_map/while
  604.8 18.2 %copy-start.5 = (bf16[1,512,768]{1,2,0:T(8,128)(2,1)S(1)}, bf16[1,512,768]{1,2,0:T(8,128)(2,1)}, u32[]{:S(2)}) copy-start(bf16[1,512,768]{1,2,0:T(8,128)(2,1)} %copy-done.4) | copy-start | bytes 2359300 | tf_op jit(solution)/shard_map/while
  650.8 18.2 %copy-start.5 = (bf16[1,512,768]{1,2,0:T(8,128)(2,1)S(1)}, bf16[1,512,768]{1,2,0:T(8,128)(2,1)}, u32[]{:S(2)}) copy-start(bf16[1,512,768]{1,2,0:T(8,128)(2,1)} %copy-done.4) | copy-start | bytes 2359300 | tf_op jit(solution)/shard_map/while
  696.9 18.2 %copy-start.5 = (bf16[1,512,768]{1,2,0:T(8,128)(2,1)S(1)}, bf16[1,512,768]{1,2,0:T(8,128)(2,1)}, u32[]{:S(2)}) copy-start(bf16[1,512,768]{1,2,0:T(8,128)(2,1)} %copy-done.4) | copy-start | bytes 2359300 | tf_op jit(solution)/shard_map/while
  742.9 18.1 %copy-start.5 = (bf16[1,512,768]{1,2,0:T(8,128)(2,1)S(1)}, bf16[1,512,768]{1,2,0:T(8,128)(2,1)}, u32[]{:S(2)}) copy-start(bf16[1,512,768]{1,2,0:T(8,128)(2,1)} %copy-done.4) | copy-start | bytes 2359300 | tf_op jit(solution)/shard_map/while
  857.3 233.6 %reduce-scatter.10.cloned.1.call-start = ((), (), s32[]{:S(2)}) async-start(), calls=%async_computation.12 | async-start | bytes 1474560 | tf_op jit(solution)/shard_map/reduce_scatter | solution.py:286
  860.4 281.0 %reduce-scatter.14.cloned.1.call-start = ((), (), s32[]{:S(2)}) async-start(), calls=%async_computation.14 | async-start | bytes 5898240 | tf_op jit(solution)/shard_map/reduce_scatter | solution.py:304
  867.4 324.4 %reduce-scatter.12.cloned.1.call-start = ((), (), s32[]{:S(2)}) async-start(), calls=%async_computation.13 | async-start | bytes 5898240 | tf_op jit(solution)/shard_map/reduce_scatter | solution.py:298
  875.4 359.3 %reduce-scatter.16.cloned.1.call-start = ((), (), s32[]{:S(2)}) async-start(), calls=%async_computation.16 | async-start | bytes 4423680 | tf_op jit(solution)/shard_map/reduce_scatter | solution.py:277
  1070.8 164.0 %copy-start.10 = (bf16[1,512,768]{2,1,0:T(8,128)(2,1)S(1)}, bf16[1,512,768]{2,1,0:T(8,128)(2,1)}, u32[]{:S(2)}) copy-start(bf16[1,512,768]{2,1,0:T(8,128)(2,1)} %param.35) | copy-start | bytes 2359300
  1070.8 165.5 %copy-start.52 = (bf16[192]{0:T(256)(128)(2,1)S(1)}, bf16[192]{0:T(256)(128)(2,1)}, u32[]{:S(2)}) copy-start(bf16[192]{0:T(256)(128)(2,1)} %param.34) | copy-start | bytes 1156
  1070.8 284.3 %all-reduce.23.cloned.1.call-start = ((), (), s32[]{:S(2)}) async-start(), calls=%async_computation.17 | async-start | bytes 5308416 | tf_op jit(solution)/shard_map/psum | solution.py:321
  1191.8 273.4 %all-gather.22.cloned.1.call-start = ((), (), s32[]{:S(2)}) async-start(), calls=%async_computation.15 | async-start | bytes 7962624 | tf_op jit(solution)/shard_map/all_gather | solution.py:318
  1358.2 41.5 %copy-start.8 = (f32[512,768]{1,0:T(8,128)S(1)}, f32[512,768]{1,0:T(8,128)}, u32[]{:S(2)}) copy-start(f32[512,768]{1,0:T(8,128)} %copy-done.7) | copy-start | bytes 4718596
  1358.2 41.5 %copy-start.27 = (f32[768]{0:T(1024)S(1)}, f32[768]{0:T(1024)}, u32[]{:S(2)}) copy-start(f32[768]{0:T(1024)} %copy-done.26) | copy-start | bytes 9220
  1358.2 41.5 %copy-start.30 = (f32[512]{0:T(512)S(1)}, f32[512]{0:T(512)}, u32[]{:S(2)}) copy-start(f32[512]{0:T(512)} %copy-done.29) | copy-start | bytes 6148
  1358.2 41.5 %copy-start.32 = (f32[512]{0:T(512)S(1)}, f32[512]{0:T(512)}, u32[]{:S(2)}) copy-start(f32[512]{0:T(512)} %copy-done.31) | copy-start | bytes 6148
  1358.2 42.7 %copy-start.12 = (f32[512,768]{1,0:T(8,128)S(1)}, f32[512,768]{1,0:T(8,128)}, u32[]{:S(2)}) copy-start(f32[512,768]{1,0:T(8,128)} %copy-done.11) | copy-start | bytes 4718596
  1358.2 42.7 %copy-start.41 = (f32[512]{0:T(512)S(1)}, f32[512]{0:T(512)}, u32[]{:S(2)}) copy-start(f32[512]{0:T(512)} %copy-done.40) | copy-start | bytes 6148
  (79 other events, 385.5 us)
Sparse Core Ops, SparseCore 0:
  9.5 33.6 all-gather.9
  50.9 98.7 all-gather.13
  152.5 96.8 all-gather.11
  250.8 15.6 all-gather.15
  267.9 37.4 all-gather.17
  306.8 37.4 all-gather.19
  857.4 205.5 reduce-scatter.7
  1066.1 24.6 reduce-scatter.9
  1093.4 47.9 reduce-scatter.13
  1143.8 47.9 reduce-scatter.11
  1194.4 40.3 reduce-scatter.15
  1238.6 116.4 all-reduce.22
  1357.3 107.9 all-gather.21
